TPU v7x, 32 devices: a whole 2x2x4 slice. The times are simulated.
32 devices in a mesh: facet: 8 (over z, y), col: 4 (over x, core).
Axes of the slice: x: 2, y: 2, z: 4, core: 2. Of those that a mesh axis runs over, the one named last changes fastest.
Arguments:
- prepared: bfloat16 [8, 2, 8192, 512], P('facet', None, None, 'col'), may hold values from -6 to 6
- sub_off: int32 [8, 4], P(None, 'col'), may hold values from 0 to 8191
- fac_off: int32 [8], replicated, may hold values from 0 to 511
- win_col: int32 [4, 128], replicated, may hold values from 0 to 255
- vis_weights: bfloat16 [8, 2, 512, 512], P('facet', None, None, 'col'), may hold values from -6 to 6
Outputs:
- facet_strips: bfloat16 [8, 2, 8192, 256], P('facet', None, 'col')
All inputs are finite; a program needn't handle non-finite values.
Results may differ from a plain program's by a relative error of at most 0.0093.
Values may be sent and summed in bfloat16 or wider, within the bound.
A program may use at most 128 MiB of HBM per device.

v0:
```python
import math

import jax
import jax.numpy as jnp
from jax import lax
from jax.sharding import PartitionSpec as P

XM = 128


def taper_curve(length):
    position = (jnp.arange(length, dtype=jnp.float32) + 0.5) / length
    return 0.3 + 0.7 * jnp.sin(math.pi * position) ** 2


def phases(row_ids, col_ids, length, sign_factor, scaling):
    products = row_ids[:, None] * col_ids[None, :] % length
    angles = 2.0 * math.pi / length * products.astype(jnp.float32)
    return (jnp.cos(angles) * scaling, sign_factor * jnp.sin(angles) * scaling)


def complex_block(real_part, imag_part):
    upper_rows = jnp.concatenate([real_part, -imag_part], axis=1)
    lower_rows = jnp.concatenate([imag_part, real_part], axis=1)
    return jnp.concatenate([upper_rows, lower_rows], axis=0).astype(jnp.bfloat16)


def small_tables(length):
    positions = jnp.arange(length, dtype=jnp.int32)
    taper_vals = taper_curve(length)
    fwd_re, fwd_im = phases(positions, positions, length, -1.0, 1.0 / math.sqrt(length))
    back_re, back_im = phases(positions, positions, length, 1.0, 1.0 / math.sqrt(length))
    forward = complex_block(fwd_re * taper_vals[None, :], fwd_im * taper_vals[None, :])
    backward = complex_block(back_re * taper_vals[:, None], back_im * taper_vals[:, None])
    return (forward, backward)


def grid_tables(length, facet_count, contrib_len):
    positions = jnp.arange(length, dtype=jnp.int32)
    fwd_re, fwd_im = phases(
        positions, positions, length, -1.0, 1.0 / math.sqrt(facet_count * contrib_len)
    )
    back_re, back_im = phases(positions, positions, length, 1.0, 1.0 / math.sqrt(length))
    return (complex_block(fwd_re, fwd_im), complex_block(back_re, back_im))


def finish_map(columns, out_cols):
    frequency = jnp.arange(out_cols, dtype=jnp.int32)
    products = columns[:, None] * frequency[None, :] % out_cols
    angles = 2.0 * math.pi / out_cols * products.astype(jnp.float32)
    scaling = 1.0 / math.sqrt(2 * out_cols)
    real_part = jnp.cos(angles) * scaling
    imag_part = jnp.sin(angles) * scaling
    from_real = jnp.concatenate([real_part, imag_part], axis=1)
    from_imag = jnp.concatenate([-imag_part, real_part], axis=1)
    return jnp.stack([from_real, from_imag], axis=0).astype(jnp.bfloat16)


def apply_weights(spectrum, weights):
    spec_re = spectrum[..., 0, :, :]
    spec_im = spectrum[..., 1, :, :]
    weight_re = weights[..., 0, :, :].astype(jnp.float32)
    weight_im = weights[..., 1, :, :].astype(jnp.float32)
    joined = jnp.stack(
        [weight_re * spec_re - weight_im * spec_im, weight_re * spec_im + weight_im * spec_re],
        axis=-3,
    )
    return joined.astype(jnp.bfloat16)


def body(prepared, sub_off, fac_off, win_col, vis_weights):
    facet_count = fac_off.shape[0]
    group_count = lax.axis_size("facet")
    per_device = vis_weights.shape[0]
    grid_len = vis_weights.shape[2]
    facet_strip = prepared[0]
    facet_len = facet_strip.shape[1]
    strip_width = facet_strip.shape[2]
    window_pos = jnp.arange(XM, dtype=jnp.int32)
    forward_small, backward_small = small_tables(XM)
    forward_grid, backward_grid = grid_tables(grid_len, facet_count, XM)
    starts = sub_off[:, 0].reshape(group_count, per_device).T
    src_rows = (starts[:, :, None] + window_pos[None, None, :]) % facet_len
    picked = (
        facet_strip[:, src_rows]
        .transpose(1, 2, 0, 3, 4)
        .reshape(per_device, group_count, 2 * XM, strip_width)
    )
    payload = jnp.einsum(
        "ab,sfbc->sfac", forward_small, picked, preferred_element_type=jnp.float32
    ).astype(jnp.bfloat16)
    arrived = lax.all_to_all(payload, "facet", split_axis=1, concat_axis=1, tiled=True)
    dest_rows = ((fac_off[:, None] + window_pos[None, :]) % grid_len).reshape(-1)
    placement = (dest_rows[None, :] == jnp.arange(grid_len, dtype=jnp.int32)[:, None]).astype(
        jnp.bfloat16
    )
    flat_rows = arrived.reshape(per_device, facet_count, 2, XM, strip_width).transpose(
        0, 2, 1, 3, 4
    )
    flat_rows = flat_rows.reshape(per_device, 2, facet_count * XM, strip_width)
    assembled = jnp.einsum(
        "rq,spqc->sprc", placement, flat_rows, preferred_element_type=jnp.float32
    ).astype(jnp.bfloat16)
    spectrum = jnp.einsum(
        "ab,sbc->sac",
        forward_grid,
        assembled.reshape(per_device, 2 * grid_len, strip_width),
        preferred_element_type=jnp.float32,
    )
    weighted = apply_weights(spectrum.reshape(per_device, 2, grid_len, strip_width), vis_weights)
    grid_image = jnp.einsum(
        "ab,sbc->sac",
        backward_grid,
        weighted.reshape(per_device, 2 * grid_len, strip_width),
        preferred_element_type=jnp.float32,
    )
    grid_image = grid_image.astype(jnp.bfloat16).reshape(per_device, 2, grid_len, strip_width)
    back_rows = (
        grid_image[:, :, dest_rows]
        .reshape(per_device, 2, facet_count, XM, strip_width)
        .transpose(0, 2, 1, 3, 4)
    )
    back_rows = back_rows.reshape(per_device, facet_count, 2 * XM, strip_width)
    returned = lax.all_to_all(back_rows, "facet", split_axis=1, concat_axis=1, tiled=True)
    item_count = per_device * group_count
    returned_terms = jnp.einsum(
        "ab,sfbc->sfac", backward_small, returned, preferred_element_type=jnp.float32
    )
    returned_terms = returned_terms.reshape(item_count, 2, XM, strip_width)
    item_starts = starts.reshape(-1)
    row_shift = item_starts % XM
    block_ids = item_starts // XM
    block_count = facet_len // XM
    padded_terms = jnp.concatenate([returned_terms, jnp.zeros_like(returned_terms)], axis=2)
    frames = jax.vmap(lambda term, amount: jnp.roll(term, amount, axis=1))(padded_terms, row_shift)
    frames = frames.reshape(item_count, 2, 2, XM, strip_width)
    block_range = jnp.arange(block_count, dtype=jnp.int32)[:, None]
    lower_hits = (block_ids[None, :] == block_range).astype(jnp.float32)
    upper_hits = (((block_ids + 1) % block_count)[None, :] == block_range).astype(jnp.float32)
    accum = jnp.einsum(
        "bs,spyc->pbyc", lower_hits, frames[:, :, 0], precision=lax.Precision.HIGHEST
    )
    accum = accum + jnp.einsum(
        "bs,spyc->pbyc", upper_hits, frames[:, :, 1], precision=lax.Precision.HIGHEST
    )
    strip_sum = accum.reshape(2, facet_len, strip_width).astype(jnp.bfloat16)
    col_count = lax.axis_size("col")
    out_cols = strip_width * col_count // 2
    own_rows = facet_len // col_count
    all_maps = jax.vmap(lambda columns: finish_map(columns, out_cols))(win_col)
    moved_rows = lax.all_to_all(strip_sum, "col", split_axis=1, concat_axis=0, tiled=True)
    moved_rows = moved_rows.reshape(col_count, 2, own_rows, strip_width)
    summed = jnp.einsum("cpyk,cpkm->ym", moved_rows, all_maps, preferred_element_type=jnp.float32)
    result = summed.astype(jnp.bfloat16).reshape(own_rows, 2, out_cols).transpose(1, 0, 2)
    return result.reshape(1, 2, own_rows, out_cols)


def solution(mesh):
    in_specs = (
        P("facet", None, None, "col"),
        P(None, "col"),
        P(),
        P(),
        P("facet", None, None, "col"),
    )
    out_specs = P("facet", None, "col", None)
    return jax.shard_map(body, mesh=mesh, in_specs=in_specs, out_specs=out_specs, check_vma=False)
```

profile of v0, /device:TPU:0, one launch (start us, length us, event | category | flops | bytes accessed | tf_op | source)
XLA Modules:
  0.0 197.0 jit_solution(260517381722625866)
XLA Ops:
  0.0 0.1 broadcast_multiply_fusion
  0.1 0.1 broadcast_multiply_fusion.1
  0.1 0.0 copy-start.3
  0.1 10.1 %copy.72 = bf16[1,2,8192,128]{3,1,2,0:T(2,128)(2,1)} copy(bf16[1,2,8192,128]{3,2,1,0:T(8,128)(2,1)} %param.5) | data formatting | bytes 8388608 | tf_op args[0]
  10.2 0.0 copy-done.3
  10.2 0.1 fusion.88
  10.3 0.0 copy-start.2
  10.3 5.9 %gather_fusion = bf16[1024,2,128]{2,1,0:T(2,128)(2,1)S(1)} fusion(bf16[2,8192,128]{2,0,1:T(2,128)(2,1)} %bitcast.141, s32[1024]{0:T(1024)S(1)} %fusion.88), kind=kCustom, calls=%fused_computation | custom fusion | bytes 1052672 | tf_op jit(solution)/shard_map/gather | solution.py:85
  16.2 2.1 %copy.33 = bf16[1,8,2,128,128]{3,2,4,1,0:T(2,128)(2,1)S(1)} copy(bf16[1,8,2,128,128]{4,2,3,1,0:T(2,128)(2,1)S(1)} %bitcast.144) | data formatting | bytes 1048576 | tf_op jit(solution)/shard_map/transpose | solution.py:86
  18.3 0.3 reshape.349
  18.6 0.3 negate_convert_fusion.3
  18.9 1.1 fusion.25
  20.1 7.3 %all-to-all-start = ((bf16[1,8,256,128]{2,3,0,1:T(8,128)(2,1)}), bf16[1,8,256,128]{2,3,0,1:T(8,128)(2,1)S(1)}, u32[]{:S(2)}, u32[]{:S(2)}) async-start(bf16[1,8,256,128]{2,3,0,1:T(8,128)(2,1)} %fusion.25), calls=%async_computation | async-start | bytes 1048576 | tf_op jit(solution)/shard_map/all_to_all | solution.py:92
  27.4 5.2 %negate_convert_fusion.1 = (bf16[512,512]{1,0:T(8,128)(2,1)S(1)}, bf16[512,512]{1,0:T(8,128)(2,1)}) fusion(), kind=kLoop, calls=%fused_computation.52 | loop fusion | flops 4980736 | bytes 1048576 | tf_op jit(solution)/shard_map/convert.27
  32.6 4.6 %multiply_convert_fusion.3 = bf16[512,512]{1,0:T(8,128)(2,1)} fusion(), kind=kLoop, calls=%fused_computation.59 | loop fusion | flops 4194304 | bytes 524288 | tf_op jit(solution)/shard_map/convert.24
  37.2 4.4 %negate_convert_fusion = (bf16[512,512]{1,0:T(8,128)(2,1)S(1)}, bf16[512,512]{1,0:T(8,128)(2,1)S(1)}) fusion(), kind=kLoop, calls=%fused_computation.50 | loop fusion | flops 4980736 | bytes 1048576 | tf_op jit(solution)/shard_map/convert.19
  41.6 4.0 %multiply_convert_fusion.2 = bf16[512,512]{1,0:T(8,128)(2,1)S(1)} fusion(), kind=kLoop, calls=%fused_computation.58 | loop fusion | flops 4194304 | bytes 524288 | tf_op jit(solution)/shard_map/convert.16
  45.6 0.0 copy-done.2
  45.6 0.1 add_select_fusion.3
  45.7 0.1 iota_add_fusion
  45.8 0.0 all-to-all-done
  45.8 0.1 reshape.350
  46.0 0.3 copy.73
  46.3 0.2 reshape.351
  46.6 0.6 fusion.35
  47.1 0.2 copy.36
  47.3 0.0 copy-start
  47.3 2.2 %fusion.26 = f32[1,1024,128]{1,2,0:T(8,128)S(1)} fusion(bf16[1024,128]{1,0:T(8,128)(2,1)S(1)} %bitcast.148, bf16[512,512]{1,0:T(8,128)(2,1)} %get-tuple-element.25, bf16[512,512]{1,0:T(8,128)(2,1)} %multiply_convert_fusion.3, bf16[512,512]{1,0:T(8,128)(2,1)S(1)} %get-tuple-element.24), kind=kOutput, calls=%fused_computation.36 | convolution fusion | flops 276824064 | bytes 2359296 | tf_op jit(solution)/shard_map/ab,sbc->sac/dot_general | solution.py:104
  49.5 0.2 copy.57
  49.7 0.0 copy-done
  49.7 0.1 fusion.62
  49.9 0.8 fusion.38
  50.7 0.2 reshape.370
  50.9 0.4 copy.39
  51.3 3.7 %gather_fusion.1 = bf16[1024,2,128]{2,1,0:T(2,128)(2,1)S(1)} fusion(bf16[2,512,128]{2,0,1:T(2,128)(2,1)S(1)} %copy.39, s32[1024]{0:T(1024)S(1)} %broadcast_clamp_fusion), kind=kCustom, calls=%fused_computation.1 | custom fusion | bytes 1052672 | tf_op jit(solution)/shard_map/gather | solution.py:119
  55.0 2.1 %copy.40 = bf16[1,8,2,128,128]{3,2,4,1,0:T(2,128)(2,1)S(1)} copy(bf16[1,8,2,128,128]{4,2,3,1,0:T(2,128)(2,1)S(1)} %bitcast.145) | data formatting | bytes 1048576 | tf_op jit(solution)/shard_map/transpose | solution.py:121
  57.1 1.1 reshape.356
  58.2 6.0 %all-to-all-start.1 = ((bf16[1,8,256,128]{2,3,0,1:T(8,128)(2,1)}), bf16[1,8,256,128]{2,3,0,1:T(8,128)(2,1)S(1)}, u32[]{:S(2)}, u32[]{:S(2)}) async-start(bf16[1,8,256,128]{2,3,0,1:T(8,128)(2,1)} %reshape.356), calls=%async_computation.1 | async-start | bytes 1048576 | tf_op jit(solution)/shard_map/all_to_all | solution.py:124
  64.2 13.9 %all-to-all-done.1 = bf16[1,8,256,128]{2,3,0,1:T(8,128)(2,1)S(1)} async-done(((bf16[1,8,256,128]{2,3,0,1:T(8,128)(2,1)}), bf16[1,8,256,128]{2,3,0,1:T(8,128)(2,1)S(1)}, u32[]{:S(2)}, u32[]{:S(2)}) %all-to-all-start.1) | async-done | bytes 524320 | tf_op jit(solution)/shard_map/all_to_all | solution.py:124
  78.2 0.3 convolution_bitcast_fusion
  78.5 0.5 reshape.358
  79.0 1.4 copy.41
  80.5 0.3 broadcast_in_dim.3
  80.7 3.5 %pad_maximum_fusion = f32[8,2,512,128]{3,1,0,2:T(2,128)} fusion(f32[8,2,128,128]{3,1,0,2:T(2,128)S(1)} %broadcast_in_dim.3, f32[8,2,128,128]{3,1,0,2:T(2,128)S(1)} %copy.41), kind=kLoop, calls=%fused_computation.5 | loop fusion | flops 3145728 | bytes 6291456 | tf_op jit(solution)/shard_map/vmap(jit(_roll_dynamic))/concatenate | solution.py:135
  84.3 5.6 %gather_fusion.2 = f32[8,2,256,128]{3,1,2,0:T(2,128)S(1)} fusion(f32[8,2,512,128]{3,1,0,2:T(2,128)} %pad_maximum_fusion, s32[8]{0:T(128)S(1)} %or_bitcast_fusion), kind=kCustom, calls=%fused_computation.2 | custom fusion | bytes 4194432 | tf_op jit(solution)/shard_map/vmap(jit(_roll_dynamic))/gather | solution.py:135
  89.8 0.2 copy.43
  90.1 0.2 fusion.108
  90.3 3.6 %fusion.46 = f32[2,128,128,64]{2,3,1,0:T(8,128)S(1)} fusion(f32[8,2,1,128,128]{4,3,2,1,0:T(8,128)S(1)} %get-tuple-element.8, s32[8]{0:T(128)S(1)} %get-tuple-element.6), kind=kOutput, calls=%fused_computation.49 | convolution fusion | flops 201327104 | bytes 9437216 | tf_op jit(solution)/shard_map/bs,spyc->pbyc/dot_general | solution.py:140
  93.8 4.7 %fusion = bf16[2,64,128,128]{3,1,2,0:T(8,128)(2,1)S(1)} fusion(f32[2,128,128,64]{2,3,1,0:T(8,128)S(1)} %fusion.46, f32[8,2,1,128,128]{4,3,2,1,0:T(8,128)S(1)} %get-tuple-element.7, s32[8]{0:T(128)S(1)} %get-tuple-element.5), kind=kOutput, calls=%fused_computation.4 | convolution fusion | flops 205521408 | bytes 13631520 | tf_op jit(solution)/shard_map/bs,spyc->pbyc/dot_general | solution.py:143
  98.6 2.7 %copy.46 = bf16[2,64,128,128]{3,2,1,0:T(8,128)(2,1)S(1)} copy(bf16[2,64,128,128]{3,1,2,0:T(8,128)(2,1)S(1)} %fusion) | data formatting | bytes 8388608 | tf_op jit(solution)/shard_map/convert_element_type | solution.py:146
  101.3 35.5 %copy.47 = bf16[2,8192,128]{2,0,1:T(2,128)(2,1)} copy(bf16[2,8192,128]{2,1,0:T(8,128)(2,1)S(1)} %bitcast.139) | data formatting | bytes 8388608 | tf_op jit(solution)/shard_map/convert_element_type | solution.py:146
  136.8 0.0 copy-start.1
  136.8 5.0 %all-to-all-start.2 = ((bf16[2,8192,128]{2,0,1:T(2,128)(2,1)}), bf16[2,8192,128]{2,0,1:T(2,128)(2,1)}, u32[]{:S(2)}, u32[]{:S(2)}) async-start(bf16[2,8192,128]{2,0,1:T(2,128)(2,1)} %copy.47), calls=%async_computation.2 | async-start | bytes 8388608 | tf_op jit(solution)/shard_map/all_to_all | solution.py:151
  141.7 0.0 copy-done.1
  141.8 2.3 %fusion.60 = (bf16[4,128,256]{1,2,0:T(8,128)(2,1)S(1)}, bf16[4,128,256]{1,2,0:T(8,128)(2,1)S(1)}, bf16[4,128,256]{1,2,0:T(8,128)(2,1)S(1)}) fusion(s32[4,128]{1,0:T(4,128)S(1)} %copy-done.1), kind=kLoop, calls=%fused_computation.78 | loop fusion | flops 2621440 | bytes 788480 | tf_op jit(solution)/shard_map/convert.7
  144.0 0.1 maximum_bitcast_fusion.2
  144.1 45.8 %all-to-all-done.2 = bf16[2,8192,128]{2,0,1:T(2,128)(2,1)} async-done(((bf16[2,8192,128]{2,0,1:T(2,128)(2,1)}), bf16[2,8192,128]{2,0,1:T(2,128)(2,1)}, u32[]{:S(2)}, u32[]{:S(2)}) %all-to-all-start.2) | async-done | bytes 4194336 | tf_op jit(solution)/shard_map/all_to_all | solution.py:151
  189.9 4.6 %bitcast_convert_fusion = bf16[2048,512]{0,1:T(8,128)(2,1)S(1)} fusion(bf16[2,4,2048,128]{3,0,2,1:T(2,128)(2,1)} %bitcast.41, bf16[1,4,128,512]{2,3,0,1:T(8,128)(2,1)S(1)} %get-tuple-element.12, bf16[1,4,128,512]{2,3,0,1:T(8,128)(2,1)S(1)} %get-tuple-element.11), kind=kOutput, calls=%fused_computation.6 | convolution fusion | flops 2149056512 | bytes 7340032 | tf_op jit(solution)/shard_map/cpyk,cpkm->ym/dot_general | solution.py:153
  194.5 2.5 %copy.51 = bf16[2048,2,256]{2,0,1:T(8,128)(2,1)} copy(bf16[2048,2,256]{0,2,1:T(8,128)(2,1)S(1)} %bitcast.142) | data formatting | bytes 4194304 | tf_op jit(solution)/shard_map/reshape | solution.py:154
  (5 shorter events, 0.1 us)
Async XLA Ops:
  0.1 10.1 %copy-start.3 = (s32[8,1]{0,1:T(1,128)S(1)}, s32[8,1]{0,1:T(1,128)}, u32[]{:S(2)}) copy-start(s32[8,1]{0,1:T(1,128)} %param.6) | copy-start | bytes 100
  10.3 35.3 %copy-start.2 = (s32[8]{0:T(128)S(1)}, s32[8]{0:T(128)}, u32[]{:S(2)}) copy-start(s32[8]{0:T(128)} %param.7) | copy-start | bytes 100
  20.1 25.8 %all-to-all-start = ((bf16[1,8,256,128]{2,3,0,1:T(8,128)(2,1)}), bf16[1,8,256,128]{2,3,0,1:T(8,128)(2,1)S(1)}, u32[]{:S(2)}, u32[]{:S(2)}) async-start(bf16[1,8,256,128]{2,3,0,1:T(8,128)(2,1)} %fusion.25), calls=%async_computation | async-start | bytes 1048576 | tf_op jit(solution)/shard_map/all_to_all | solution.py:92
  47.3 2.4 %copy-start = (bf16[1,2,512,128]{3,2,1,0:T(8,128)(2,1)S(1)}, bf16[1,2,512,128]{3,2,1,0:T(8,128)(2,1)}, u32[]{:S(2)}) copy-start(bf16[1,2,512,128]{3,2,1,0:T(8,128)(2,1)} %param.9) | copy-start | bytes 786436
  58.2 20.0 %all-to-all-start.1 = ((bf16[1,8,256,128]{2,3,0,1:T(8,128)(2,1)}), bf16[1,8,256,128]{2,3,0,1:T(8,128)(2,1)S(1)}, u32[]{:S(2)}, u32[]{:S(2)}) async-start(bf16[1,8,256,128]{2,3,0,1:T(8,128)(2,1)} %reshape.356), calls=%async_computation.1 | async-start | bytes 1048576 | tf_op jit(solution)/shard_map/all_to_all | solution.py:124
  136.8 5.0 %copy-start.1 = (s32[4,128]{1,0:T(4,128)S(1)}, s32[4,128]{1,0:T(4,128)}, u32[]{:S(2)}) copy-start(s32[4,128]{1,0:T(4,128)} %param.8) | copy-start | bytes 6148
  136.8 53.2 %all-to-all-start.2 = ((bf16[2,8192,128]{2,0,1:T(2,128)(2,1)}), bf16[2,8192,128]{2,0,1:T(2,128)(2,1)}, u32[]{:S(2)}, u32[]{:S(2)}) async-start(bf16[2,8192,128]{2,0,1:T(2,128)(2,1)} %copy.47), calls=%async_computation.2 | async-start | bytes 8388608 | tf_op jit(solution)/shard_map/all_to_all | solution.py:151
where the time goes:
time: 198 us; the launch traced here: 197 us
  local copies, waits for them, and re-layouts  75.8 us (38%)
  waiting for transfers between devices  59.7 us (30%)
  other arithmetic  24.9 us (13%)
  starting transfers between devices  18.3 us (9%)
  matrix products  17.9 us (9%)
    all_to_all x1, waiting for transfers between devices, body(): lax.all_to_all(strip_sum, 'col', split_axis=1, concat_axis=0, tiled=True)  45.8 us
    convert_element_type x2, local copies, waits for them, and re-layouts, body(): strip_sum = accum.reshape(2, facet_len, strip_width).astype(jnp.bfloat16)  38.2 us
    another operation x7, other arithmetic  20.9 us
    all_to_all x1, waiting for transfers between devices, body(): lax.all_to_all(back_rows, 'facet', split_axis=1, concat_axis=1, tiled=True)  13.9 us
    unnamed x9, local copies, waits for them, and re-layouts  10.1 us
    all_to_all x1, starting transfers between devices, body(): lax.all_to_all(payload, 'facet', split_axis=1, concat_axis=1, tiled=True)  7.31 us
    all_to_all x1, starting transfers between devices, body(): lax.all_to_all(back_rows, 'facet', split_axis=1, concat_axis=1, tiled=True)  6 us
    gather x1, local copies, waits for them, and re-layouts, body(): facet_strip[:, src_rows].transpose(1, 2, 0, 3, 4)  5.88 us
  transfers between devices with their start and end apart: 3, of which 2 were waited for; matrix products, arithmetic and copies ran while one was open for 11% of the time, Pallas kernels for 0%

commit v1 on v0

v1 whole, which is shorter than its diff:
```python
import functools
import math

import jax
import jax.numpy as jnp
import numpy as np
from jax import lax
from jax.experimental import pallas as pl
from jax.experimental.pallas import tpu as pltpu
from jax.sharding import PartitionSpec as P

XM = 128
ALIGN = 16
MESH = pl.DeviceIdType.MESH
F32 = jnp.float32
BF16 = jnp.bfloat16


def dft(length, sign, scaling):
    ids = np.arange(length)
    angles = 2.0 * np.pi / length * (ids[:, None] * ids[None, :] % length)
    return np.cos(angles) * scaling, sign * np.sin(angles) * scaling


def stacked(real_part, imag_part, axis):
    return np.concatenate([real_part, imag_part], axis=axis).astype(jnp.bfloat16)


def window_tables(length):
    taper = 0.3 + 0.7 * np.sin(np.pi * (np.arange(length) + 0.5) / length) ** 2
    scaling = 1.0 / math.sqrt(length)
    fwd_re, fwd_im = dft(length, -1.0, scaling)
    back_re, back_im = dft(length, 1.0, scaling)
    forward = stacked(fwd_re * taper[None, :], fwd_im * taper[None, :], 0)
    backward = stacked(back_re * taper[:, None], back_im * taper[:, None], 1)
    return forward, backward


def mm(a, b):
    return jnp.dot(a, b, preferred_element_type=F32)


def iota(shape, dim):
    return lax.broadcasted_iota(jnp.int32, shape, dim)


def complex_mm(table, values, conj=False):
    prod = mm(table, values)
    n = prod.shape[0] // 2
    w = prod.shape[1] // 2
    rr, ri = prod[:n, :w], prod[:n, w:]
    ir, ii = prod[n:, :w], prod[n:, w:]
    if conj:
        return rr + ii, ri - ir
    return rr - ii, ri + ir


def exchange_kernel(
    nf, ncol, starts, fac, starts_row, prep, wts, fwd, qtab,
    terms, starts_all,
    pv, qv, wv, send1, recv1, acc, grid, send2,
    ld, s1, r1, s2, sx, sp, rt, ss, rs,
):
    me = lax.axis_index("facet")
    c = lax.axis_index("col")
    nx = ncol // 2
    xq, core = lax.div(c, 2), lax.rem(c, 2)
    partner = xq * 2 + 1 - core
    pow2 = nf & (nf - 1) == 0
    blocks = prep.shape[1]
    xa = wts.shape[1]
    chunks = 8
    step = blocks // chunks

    def peer(i):
        if not pow2:
            return lax.rem(me + i, nf)
        out, b = 0, 1
        while b < nf:
            mb, ib = lax.rem(lax.div(me, b), 2), lax.rem(lax.div(i, b), 2)
            out = out + b * (mb + ib - 2 * mb * ib)
            b *= 2
        return out

    def source(i):
        return peer(i) if pow2 else lax.rem(me + nf - i, nf)

    barrier = pltpu.get_barrier_semaphore()

    @pl.loop(1, nf)
    def _(i):
        pl.semaphore_signal(barrier, inc=1, device_id={"facet": peer(i)}, device_id_type=MESH)

    for i in range(1, ncol):
        pl.semaphore_signal(
            barrier, inc=1, device_id={"col": lax.rem(c + i, ncol)}, device_id_type=MESH
        )

    loads = [
        pltpu.make_async_copy(
            prep.at[:, pl.ds(k * step, step)], pv.at[:, pl.ds(k * step, step)], ld.at[k]
        )
        for k in range(chunks)
    ]
    q_load = pltpu.make_async_copy(qtab, qv, ld.at[chunks])
    w_load = pltpu.make_async_copy(wts, wv, ld.at[chunks + 1])
    own_starts = pltpu.make_async_copy(starts_row, starts_all.at[c], ld.at[chunks + 2])
    for copy in loads:
        copy.start()
    own_starts.start()
    q_load.start()
    w_load.start()

    def remote(src, dst, send, recv, **where):
        return pltpu.make_async_remote_copy(
            src_ref=src, dst_ref=dst, send_sem=send, recv_sem=recv,
            device_id=where, device_id_type=MESH,
        )

    def send_first(j):
        return remote(send1.at[j], recv1.at[me], s1.at[j], r1.at[me], facet=j)

    def recv_first(j):
        return remote(send1.at[j], recv1.at[j], s1.at[j], r1.at[j], facet=j)

    def send_second(j):
        return remote(send2.at[j], terms.at[c, me], s2.at[j], rt.at[c, me], facet=j)

    def arrival(cc, j):
        return remote(send2.at[j], terms.at[cc, j], s2.at[j], rt.at[cc, j], facet=j)

    def forward_x(src, j, q):
        return remote(
            src, terms.at[c, j], sx.at[q, j], rt.at[c, j], col=lax.rem(xq + q, nx) * 2 + core
        )

    def forward_partner(src, cc, j):
        return remote(src, terms.at[cc, j], sp.at[cc, j], rt.at[cc, j], col=partner)

    row_k = iota((XM, 2 * XM), 0)
    row_r = iota((XM, 2 * XM), 1)
    fwd_table = fwd[...]

    def contribution(j):
        start = starts[j]
        block = lax.div(start, XM)
        shift = lax.rem(start, XM)
        above = lax.rem(block + 1, blocks)
        top = jnp.concatenate([pv[0, block], pv[1, block]], axis=1)
        low = jnp.concatenate([pv[0, above], pv[1, above]], axis=1)
        pick = jnp.where(row_r == row_k + shift, 1.0, 0.0).astype(BF16)
        picked = mm(pick, jnp.concatenate([top, low], axis=0)).astype(BF16)
        re, im = complex_mm(fwd_table, picked)
        return jnp.concatenate([re, im], axis=1).astype(BF16)

    for copy in loads:
        copy.wait()
    pl.semaphore_wait(barrier, nf - 1 + ncol - 1)

    @pl.loop(1, nf)
    def _(i):
        j = peer(nf - i)
        send1[j] = contribution(j)
        send_first(j).start()

    recv1[me] = contribution(me)

    start_sends = []
    for i in range(1, ncol):
        to = lax.rem(c + i, ncol)
        start_sends.append(
            remote(starts_row, starts_all.at[c], ss.at[i], rs.at[c], col=to)
        )
        start_sends[-1].start()

    grid_r = iota((xa, XM), 0)
    grid_k = iota((xa, XM), 1)

    def place(j):
        hit = grid_r == lax.rem(fac[j] + grid_k, xa)
        return mm(jnp.where(hit, 1.0, 0.0).astype(BF16), recv1[j])

    acc[...] = place(me)

    @pl.loop(1, nf)
    def _(i):
        j = source(nf - i)
        recv_first(j).wait_recv()
        acc[...] += place(j)

    q_load.wait()
    w_load.wait()
    table = qv[...]
    spec_re, spec_im = complex_mm(table, acc[...].astype(BF16))
    w_re, w_im = wv[0].astype(F32), wv[1].astype(F32)
    weighted = jnp.concatenate(
        [w_re * spec_re - w_im * spec_im, w_re * spec_im + w_im * spec_re], axis=1
    ).astype(BF16)
    img_re, img_im = complex_mm(table, weighted, conj=True)
    gain = image_gain(nf, xa)
    grid[...] = (jnp.concatenate([img_re, img_im], axis=1) * gain).astype(BF16)

    back_k = iota((XM, xa), 0)
    back_r = iota((XM, xa), 1)

    def back(j):
        hit = back_r == lax.rem(fac[j] + back_k, xa)
        return mm(jnp.where(hit, 1.0, 0.0).astype(BF16), grid[...]).astype(BF16)

    send2[me] = back(me)
    own_copy = pltpu.make_async_copy(send2.at[me], terms.at[c, me], ld.at[chunks + 3])
    own_copy.start()
    for q in range(1, nx):
        forward_x(send2.at[me], me, q).start()
    forward_partner(send2.at[me], c, me).start()

    @pl.loop(1, nf)
    def _(i):
        j = peer(nf - i)
        send2[j] = back(j)
        send_second(j).start()

    def relay(j):
        for q in range(1, nx):
            cc = lax.rem(xq + nx - q, nx) * 2 + core
            arrival(cc, j).wait_recv()
            forward_partner(terms.at[cc, j], cc, j).start()

    @pl.loop(1, nf)
    def _(i):
        j = source(nf - i)
        arrival(c, j).wait_recv()
        for q in range(1, nx):
            forward_x(terms.at[c, j], j, q).start()
        forward_partner(terms.at[c, j], c, j).start()

        @pl.when(i == 2)
        def _():
            relay(me)

        @pl.when(i > 2)
        def _():
            relay(source(nf - i + 2))

    if nf == 2:
        relay(me)
    for i in range(max(1, nf - 2), nf):
        relay(source(nf - i))

    own_copy.wait()
    own_starts.wait()
    for i in range(1, ncol):
        start_sends[i - 1].wait_send()
        frm = lax.rem(c + ncol - i, ncol)
        remote(starts_row, starts_all.at[frm], ss.at[i], rs.at[frm], col=frm).wait_recv()

    @pl.loop(0, nf)
    def _(j):
        for q in range(nx):
            cc = lax.rem(xq + q, nx) * 2 + 1 - core
            arrival(cc, j).wait_recv()
            forward_partner(terms.at[c, j], lax.rem(xq + q, nx) * 2 + core, j).wait_send()
        for q in range(1, nx):
            forward_x(terms.at[c, j], j, q).wait_send()

    @pl.loop(1, nf)
    def _(i):
        j = peer(i)
        send_first(j).wait_send()
        send_second(j).wait_send()


def image_gain(nf, xa):
    return math.sqrt(nf * XM) / math.sqrt(xa)


def finish_kernel(
    nf, ncol, starts_all, win, bwd, fmap, terms, out, tv, acc, maps, stage, tsem, osem
):
    c = lax.axis_index("col")
    own_rows = out.shape[1]
    oc = out.shape[2]
    total = own_rows * ncol
    base = c * own_rows
    count = ncol * nf

    def offset(t):
        cc, j = lax.div(t, nf), lax.rem(t, nf)
        rel = starts_all[cc, 0, j] - base + XM
        rel = jnp.where(rel < 0, rel + total, rel)
        rel = jnp.where(rel >= total, rel - total, rel)
        return cc, j, rel

    def fetch(t, cc, j):
        return pltpu.make_async_copy(terms.at[cc, j], tv.at[t], tsem.at[t])

    @pl.loop(0, count)
    def _(t):
        cc, j, rel = offset(t)

        @pl.when(rel < own_rows + XM)
        def _():
            fetch(t, cc, j).start()

    fm = fmap[...]
    col_n = iota((oc, XM), 0)
    for k in range(ncol):
        hit = jnp.where(col_n == win[k : k + 1, :], 1.0, 0.0).astype(BF16)
        m = lax.dot_general(
            hit, fm, (((0,), (0,)), ((), ())), preferred_element_type=F32
        )
        m_re, m_im = m[:, :oc], m[:, oc:]
        upper = jnp.concatenate([m_re, m_im], axis=1)
        lower = jnp.concatenate([-m_im, m_re], axis=1)
        maps[k] = jnp.concatenate([upper, lower], axis=0).astype(BF16)

    acc[...] = jnp.zeros_like(acc)
    table = bwd[...]
    slot_r = iota((XM + ALIGN, XM), 0)
    slot_k = iota((XM + ALIGN, XM), 1)

    @pl.loop(0, count)
    def _(t):
        cc, j, rel = offset(t)

        @pl.when(rel < own_rows + XM)
        def _():
            fetch(t, cc, j).wait()
            moved = mm(jnp.where(slot_r == slot_k + lax.rem(rel, ALIGN), 1.0, 0.0).astype(BF16), table)
            moved = jnp.concatenate([moved[:, :XM], moved[:, XM:]], axis=0).astype(BF16)
            re, im = complex_mm(moved, tv[t])
            strip = jnp.concatenate([re, im], axis=1).astype(BF16)
            low = pl.multiple_of(lax.div(rel, ALIGN) * ALIGN, ALIGN)
            acc[pl.ds(low, XM + ALIGN), :] += mm(strip, maps[cc])

    chunk = own_rows // osem.shape[0]
    copies = []
    for k in range(osem.shape[0]):
        rows = pl.ds(k * chunk, chunk)
        src = pl.ds(XM + k * chunk, chunk)
        stage[0, rows, :] = acc[src, :oc].astype(BF16)
        stage[1, rows, :] = acc[src, oc:].astype(BF16)
        copy = pltpu.make_async_copy(stage.at[:, rows, :], out.at[:, rows, :], osem.at[k])
        copy.start()
        copies.append(copy)
    for copy in copies:
        copy.wait()


def body(prepared, sub_off, fac_off, win_col, vis_weights):
    nf = fac_off.shape[0]
    ncol = lax.axis_size("col")
    facet_strip = prepared[0]
    facet_len, width = facet_strip.shape[1:]
    strip_blocks = facet_strip.reshape(2, facet_len // XM, XM, width)
    weights = vis_weights[0]
    xa = weights.shape[1]
    oc = width * ncol // 2
    own_rows = facet_len // ncol
    starts = sub_off[:, 0]
    lanes = -(-nf // 128) * 128
    starts_row = jnp.broadcast_to(jnp.pad(starts, (0, lanes - nf))[None, :], (8, lanes))

    forward, backward = window_tables(XM)
    q_table = stacked(*dft(xa, -1.0, 1.0 / math.sqrt(nf * XM)), 0)
    out_map = stacked(*dft(oc, 1.0, 1.0 / math.sqrt(2 * oc)), 1)

    smem = pl.BlockSpec(memory_space=pltpu.SMEM)
    vmem = pl.BlockSpec(memory_space=pltpu.VMEM)
    hbm = pl.BlockSpec(memory_space=pl.ANY)
    dma = pltpu.SemaphoreType.DMA
    terms, starts_all = pl.pallas_call(
        functools.partial(exchange_kernel, nf, ncol),
        out_shape=(
            jax.ShapeDtypeStruct((ncol, nf, XM, 2 * width), BF16),
            jax.ShapeDtypeStruct((ncol, 8, lanes), jnp.int32),
        ),
        in_specs=[smem, smem, hbm, hbm, hbm, vmem, hbm],
        out_specs=(hbm, hbm),
        scratch_shapes=[
            pltpu.VMEM(strip_blocks.shape, BF16),
            pltpu.VMEM(q_table.shape, BF16),
            pltpu.VMEM(weights.shape, BF16),
            pltpu.VMEM((nf, XM, 2 * width), BF16),
            pltpu.VMEM((nf, XM, 2 * width), BF16),
            pltpu.VMEM((xa, 2 * width), F32),
            pltpu.VMEM((xa, 2 * width), BF16),
            pltpu.VMEM((nf, XM, 2 * width), BF16),
            dma((12,)), dma((nf,)), dma((nf,)), dma((nf,)),
            dma((ncol, nf)), dma((ncol, nf)), dma((ncol, nf)), dma((ncol,)), dma((ncol,)),
        ],
        compiler_params=pltpu.CompilerParams(collective_id=0, has_side_effects=True),
        name="exchange",
    )(starts, fac_off, starts_row, strip_blocks, weights, jnp.asarray(forward), jnp.asarray(q_table))
    out = pl.pallas_call(
        functools.partial(finish_kernel, nf, ncol),
        out_shape=jax.ShapeDtypeStruct((2, own_rows, oc), BF16),
        in_specs=[smem, vmem, vmem, vmem, hbm],
        out_specs=hbm,
        scratch_shapes=[
            pltpu.VMEM((ncol * nf, XM, 2 * width), BF16),
            pltpu.VMEM((own_rows + 2 * XM + ALIGN, 2 * oc), F32),
            pltpu.VMEM((ncol, 2 * width, 2 * oc), BF16),
            pltpu.VMEM((2, own_rows, oc), BF16),
            dma((ncol * nf,)),
            dma((4,)),
        ],
        name="finish",
    )(starts_all, win_col, jnp.asarray(backward), jnp.asarray(out_map), terms)
    return out[None]


def solution(mesh):
    in_specs = (
        P("facet", None, None, "col"),
        P(None, "col"),
        P(),
        P(),
        P("facet", None, None, "col"),
    )
    out_specs = P("facet", None, "col", None)
    return jax.shard_map(body, mesh=mesh, in_specs=in_specs, out_specs=out_specs, check_vma=False)
```

time: 198 us -> 53.9 us (0.27)
  the two profiles are of different devices: /device:TPU:0 before, /device:TPU:1 now
where the time goes in v1:
time: 53.9 us; the launch traced here: 54.4 us
  Pallas kernels  53.2 us (99%)
  local copies, waits for them, and re-layouts  1.25 us (2%)
    pallas_call x1, Pallas kernels, body(): pl.pallas_call(functools.partial(exchange_kernel, nf, ncol), out_shape=(j...  42.6 us
    pallas_call x1, Pallas kernels, body(): pl.pallas_call(functools.partial(finish_kernel, nf, ncol), out_shape=jax....  10.6 us

profile of v1, /device:TPU:1, one launch (start us, length us, event | category | flops | bytes accessed | tf_op | source)
XLA Modules:
  0.0 54.4 jit_solution(13659093595037581459)
XLA Ops:
  0.0 0.7 %pad.4 = s32[128]{0:T(128)S(1)} pad(s32[8]{0:T(128)} %bitcast.6, s32[]{:T(128)} %constant.4.clone.1), padding=0_120 | pad | bytes 548 | tf_op jit(solution)/shard_map/jit(_pad)/pad | solution.py:362
  0.7 0.6 %broadcast_in_dim.4.starts_row = s32[8,128]{1,0:T(8,128)} broadcast(s32[128]{0:T(128)S(1)} %pad.4), dimensions={1} | broadcast | bytes 4608 | tf_op jit(solution)/shard_map/broadcast_in_dim | solution.py:362
  1.3 42.6 %exchange.1 = (bf16[4,8,128,256]{3,2,1,0:T(8,128)(2,1)}, s32[4,8,128]{2,1,0:T(8,128)}) custom-call(s32[8]{0:T(128)} %bitcast.7, s32[8]{0:T(128)} %fac.1, s32[8,128]{1,0:T(8,128)} %broadcast_in_dim.4.starts_row, bf16[2,64,128,128]{3,2,1,0:T(8,128)(2,1)} %bitcast.4, bf16[2,512,128]{2,1,0:T(8,128)(2,1)} %bitcast.5, bf16[256,128]{1,0:T(8,128)(2,1)} %constant.10.clone.fwd, ...), custom_call_target="tpu_custom_call" | custom-call | tf_op jit(solution)/shard_map/exchange/pallas_call | solution.py:372
  43.9 10.6 %finish.1 = bf16[2,2048,256]{2,1,0:T(8,128)(2,1)} custom-call(s32[4,8,128]{2,1,0:T(8,128)} %get-tuple-element.7.starts_all, s32[4,128]{1,0:T(4,128)} %win.1, bf16[128,256]{1,0:T(8,128)(2,1)} %constant.12.clone.bwd, bf16[256,512]{1,0:T(8,128)(2,1)} %constant.13.clone.fmap, bf16[4,8,128,256]{3,2,1,0:T(8,128)(2,1)} %get-tuple-element.8.terms), custom_call_target="tpu_custom_call" | custom-call | tf_op jit(solution)/shard_map/finish/pallas_call | solution.py:395

commit v2 on v1

v2 whole, which is shorter than its diff:
```python
import functools
import math

import jax
import jax.numpy as jnp
import numpy as np
from jax import lax
from jax.experimental import pallas as pl
from jax.experimental.pallas import tpu as pltpu
from jax.sharding import PartitionSpec as P

XM = 128
ALIGN = 16
CHUNKS = 8
OUT_CHUNKS = 8
LAG = 3
MESH = pl.DeviceIdType.MESH
F32 = jnp.float32
BF16 = jnp.bfloat16


def dft(length, sign, scaling):
    ids = np.arange(length)
    angles = 2.0 * np.pi / length * (ids[:, None] * ids[None, :] % length)
    return np.cos(angles) * scaling, sign * np.sin(angles) * scaling


def stacked(real_part, imag_part, axis):
    return np.concatenate([real_part, imag_part], axis=axis).astype(jnp.bfloat16)


def window_tables(length):
    taper = 0.3 + 0.7 * np.sin(np.pi * (np.arange(length) + 0.5) / length) ** 2
    scaling = 1.0 / math.sqrt(length)
    fwd_re, fwd_im = dft(length, -1.0, scaling)
    back_re, back_im = dft(length, 1.0, scaling)
    forward = stacked(fwd_re * taper[None, :], fwd_im * taper[None, :], 0)
    backward = stacked(back_re * taper[:, None], back_im * taper[:, None], 1)
    return forward, backward


def mm(a, b):
    return jnp.dot(a, b, preferred_element_type=F32)


def iota(shape, dim):
    return lax.broadcasted_iota(jnp.int32, shape, dim)


def one_hot(hit):
    return jnp.where(hit, 1.0, 0.0).astype(BF16)


def exchange_kernel(
    nf, ncol, starts, fac, prep, wts, fwd, bwd, win, fmap, qtab,
    terms, starts_all, maps_out,
    pv, qv, wv, send1, recv1, acc, grid, send2, ctab, maps, svec, fv, wdup,
    ld, s1, r1, s2, sx, sp, rt, ss, rs,
):
    me = lax.axis_index("facet")
    c = lax.axis_index("col")
    nx = ncol // 2
    xq, core = lax.div(c, 2), lax.rem(c, 2)
    partner = xq * 2 + 1 - core
    pow2 = nf & (nf - 1) == 0
    blocks = prep.shape[1]
    xa, width = wts.shape[1:]
    half = width // 2
    oc = fmap.shape[0]
    chunks = CHUNKS
    step = blocks // chunks

    def peer(i):
        if not pow2:
            return lax.rem(me + i, nf)
        out, b = 0, 1
        while b < nf:
            mb, ib = lax.rem(lax.div(me, b), 2), lax.rem(lax.div(i, b), 2)
            out = out + b * (mb + ib - 2 * mb * ib)
            b *= 2
        return out

    def source(i):
        return peer(i) if pow2 else lax.rem(me + nf - i, nf)

    barrier = pltpu.get_barrier_semaphore()

    @pl.loop(1, nf)
    def _(i):
        pl.semaphore_signal(barrier, inc=1, device_id={"facet": peer(i)}, device_id_type=MESH)

    for i in range(1, ncol):
        pl.semaphore_signal(
            barrier, inc=1, device_id={"col": lax.rem(c + i, ncol)}, device_id_type=MESH
        )

    loads = [
        pltpu.make_async_copy(
            prep.at[:, pl.ds(k * step, step)], pv.at[:, pl.ds(k * step, step)], ld.at[k]
        )
        for k in range(chunks)
    ]
    w_load = pltpu.make_async_copy(wts, wv, ld.at[chunks])
    q_load = pltpu.make_async_copy(qtab, qv, ld.at[chunks + 1])
    f_load = pltpu.make_async_copy(fmap, fv, ld.at[chunks + 2])
    for copy in loads:
        copy.start()
    w_load.start()
    q_load.start()
    f_load.start()

    lane = iota(svec.shape, 1)
    row = jnp.zeros(svec.shape, jnp.int32)
    svec[...] = lax.fori_loop(0, nf, lambda j, v: jnp.where(lane == j, starts[j], v), row)

    def remote(src, dst, send, recv, **where):
        return pltpu.make_async_remote_copy(
            src_ref=src, dst_ref=dst, send_sem=send, recv_sem=recv,
            device_id=where, device_id_type=MESH,
        )

    def send_first(h, j):
        return remote(send1.at[h, j], recv1.at[h, me], s1.at[h, j], r1.at[h, me], facet=j)

    def recv_first(h, j):
        return remote(send1.at[h, j], recv1.at[h, j], s1.at[h, j], r1.at[h, j], facet=j)

    def send_second(h, j):
        return remote(send2.at[h, j], terms.at[c, me, h], s2.at[h, j], rt.at[c, me, h], facet=j)

    def arrival(cc, j, h):
        return remote(send2.at[h, j], terms.at[cc, j, h], s2.at[h, j], rt.at[cc, j, h], facet=j)

    def forward_x(src, j, h, q):
        return remote(
            src, terms.at[c, j, h], sx.at[q, j, h], rt.at[c, j, h],
            col=lax.rem(xq + q, nx) * 2 + core,
        )

    def forward_partner(src, cc, j, h):
        return remote(src, terms.at[cc, j, h], sp.at[cc, j, h], rt.at[cc, j, h], col=partner)

    row_k = iota((XM, 2 * XM), 0)
    row_r = iota((XM, 2 * XM), 1)
    fwd_table = fwd[...]

    def contribution(j, dst):
        start = starts[j]
        block = lax.div(start, XM)
        shift = lax.rem(start, XM)
        above = lax.rem(block + 1, blocks)
        top = jnp.concatenate([pv[0, block], pv[1, block]], axis=1)
        low = jnp.concatenate([pv[0, above], pv[1, above]], axis=1)
        picked = mm(one_hot(row_r == row_k + shift), jnp.concatenate([top, low], axis=0))
        prod = mm(fwd_table, picked.astype(BF16))
        re = prod[:XM, :width] - prod[XM:, width:]
        im = prod[:XM, width:] + prod[XM:, :width]
        first = iota(re.shape, 1) < half
        dst[0, j] = jnp.where(first, re, pltpu.roll(im, half, 1)).astype(BF16)
        dst[1, j] = jnp.where(first, pltpu.roll(re, half, 1), im).astype(BF16)

    for copy in loads:
        copy.wait()
    pl.semaphore_wait(barrier, nf - 1 + ncol - 1)

    @pl.loop(1, nf)
    def _(i):
        j = peer(nf - i)
        contribution(j, send1)
        send_first(0, j).start()

    @pl.loop(1, nf)
    def _(i):
        send_first(1, peer(nf - i)).start()

    contribution(me, recv1)

    start_sends = []
    for i in range(1, ncol):
        to = lax.rem(c + i, ncol)
        start_sends.append(remote(svec, starts_all.at[c], ss.at[i], rs.at[c], col=to))
        start_sends[-1].start()
    own_starts = pltpu.make_async_copy(svec, starts_all.at[c], ld.at[chunks + 3])
    own_starts.start()

    turn = iota((XM, XM), 0) == lax.rem(iota((XM, XM), 1) + lax.rem(starts[me], ALIGN), XM)
    turned = mm(one_hot(turn), bwd[...]).astype(BF16)
    turned = jnp.concatenate([turned[:, :XM], turned[:, XM:]], axis=0)
    back_k = iota((XM, xa), 0)
    back_r = iota((XM, xa), 1)

    @pl.loop(0, nf)
    def _(j):
        hit = back_r == lax.rem(fac[j] + back_k, xa)
        ctab[j] = mm(turned, one_hot(hit)).astype(BF16)

    w_load.wait()
    near = iota((xa, width), 1) < half
    for p in range(2):
        w = wv[p].astype(F32)
        swapped = pltpu.roll(w, half, 1)
        wdup[0, p] = jnp.where(near, w, swapped)
        wdup[1, p] = jnp.where(near, swapped, w)

    grid_r = iota((xa, XM), 0)
    grid_k = iota((xa, XM), 1)

    def place(h, j):
        hit = grid_r == lax.rem(fac[j] + grid_k, xa)
        return mm(one_hot(hit), recv1[h, j])

    def twist(prod, conj):
        n = prod.shape[0] // 2
        crossed = pltpu.roll(prod[n:], half, 1)
        first = iota(crossed.shape, 1) < half
        minus = jnp.logical_not(first) if conj else first
        return prod[:n] + jnp.where(minus, -crossed, crossed)

    def window_maps():
        f_load.wait()
        fm = fv[...]
        col_n = iota((oc, width), 0)
        for k in range(ncol):
            m = lax.dot_general(
                one_hot(col_n == win[k : k + 1, :]), fm, (((0,), (0,)), ((), ())),
                preferred_element_type=F32,
            ).astype(BF16)
            m_re, m_im = m[:, :oc], m[:, oc:]
            upper = jnp.concatenate([m_re, m_im], axis=1)
            lower = jnp.concatenate([-m_im, m_re], axis=1)
            maps[k] = jnp.concatenate(
                [upper[:half], lower[:half], upper[half:], lower[half:]], axis=0
            )

    own_copies = []
    map_copy = pltpu.make_async_copy(maps, maps_out, ld.at[chunks + 4])
    for h in range(2):
        acc[...] = place(h, me)

        @pl.loop(1, nf)
        def _(i):
            j = source(nf - i)
            recv_first(h, j).wait_recv()
            acc[...] += place(h, j)

        if h == 0:
            q_load.wait()
        table = qv[...]
        spectrum = twist(mm(table, acc[...].astype(BF16)), False)
        crossed = wdup[h, 1] * pltpu.roll(spectrum, half, 1)
        weighted = wdup[h, 0] * spectrum + jnp.where(near, -crossed, crossed)
        image = twist(mm(table, weighted.astype(BF16)), True)
        grid[...] = (image * image_gain(nf, xa)).astype(BF16)

        def back(j):
            return twist(mm(ctab[j], grid[...]), False).astype(BF16)

        send2[h, me] = back(me)
        copy = pltpu.make_async_copy(
            send2.at[h, me], terms.at[c, me, h], ld.at[chunks + 5 + h]
        )
        copy.start()
        own_copies.append(copy)
        for q in range(1, nx):
            forward_x(send2.at[h, me], me, h, q).start()
        forward_partner(send2.at[h, me], c, me, h).start()

        @pl.loop(1, nf)
        def _(i):
            j = peer(nf - i)
            send2[h, j] = back(j)
            send_second(h, j).start()

        if h == 0:
            window_maps()
            map_copy.start()

    def relay(u):
        h, j = lax.div(u, nf), source(nf - lax.rem(u, nf))
        for q in range(1, nx):
            cc = lax.rem(xq + nx - q, nx) * 2 + core
            arrival(cc, j, h).wait_recv()
            forward_partner(terms.at[cc, j, h], cc, j, h).start()

    @pl.loop(0, 2 * nf)
    def _(u):
        h, i = lax.div(u, nf), lax.rem(u, nf)

        @pl.when(i > 0)
        def _():
            j = source(nf - i)
            arrival(c, j, h).wait_recv()
            for q in range(1, nx):
                forward_x(terms.at[c, j, h], j, h, q).start()
            forward_partner(terms.at[c, j, h], c, j, h).start()

        @pl.when(u >= LAG)
        def _():
            relay(u - LAG)

    @pl.loop(2 * nf - LAG, 2 * nf)
    def _(u):
        relay(u)

    for copy in own_copies:
        copy.wait()
    own_starts.wait()
    map_copy.wait()
    for i in range(1, ncol):
        start_sends[i - 1].wait_send()
        frm = lax.rem(c + ncol - i, ncol)
        remote(svec, starts_all.at[frm], ss.at[i], rs.at[frm], col=frm).wait_recv()

    @pl.loop(0, nf)
    def _(j):
        for h in range(2):
            for q in range(nx):
                cc = lax.rem(xq + q, nx) * 2 + 1 - core
                arrival(cc, j, h).wait_recv()
                mine = lax.rem(xq + q, nx) * 2 + core
                forward_partner(terms.at[c, j, h], mine, j, h).wait_send()
            for q in range(1, nx):
                forward_x(terms.at[c, j, h], j, h, q).wait_send()

    @pl.loop(1, nf)
    def _(i):
        j = peer(i)
        for h in range(2):
            send_first(h, j).wait_send()
            send_second(h, j).wait_send()


def image_gain(nf, xa):
    return math.sqrt(nf * XM) / math.sqrt(xa)


def finish_kernel(nf, ncol, starts_all, terms, maps_in, out, tv, acc, maps, stage, tsem, osem):
    c = lax.axis_index("col")
    own_rows = out.shape[1]
    oc = out.shape[2]
    total = own_rows * ncol
    base = c * own_rows
    count = ncol * nf

    def offset(t):
        cc, j = lax.div(t, nf), lax.rem(t, nf)
        rel = starts_all[cc, 0, j] - base + XM
        rel = jnp.where(rel < 0, rel + total, rel)
        rel = jnp.where(rel >= total, rel - total, rel)
        return cc, j, rel

    def fetch(t, cc, j):
        return pltpu.make_async_copy(terms.at[cc, j], tv.at[t], tsem.at[t])

    map_load = pltpu.make_async_copy(maps_in, maps, tsem.at[count])
    map_load.start()

    @pl.loop(0, count)
    def _(t):
        cc, j, rel = offset(t)

        @pl.when(rel < own_rows + XM)
        def _():
            fetch(t, cc, j).start()

    acc[...] = jnp.zeros_like(acc)
    slot = iota((XM, 2 * oc), 0)
    edge = iota((ALIGN, 2 * oc), 0)
    map_load.wait()

    @pl.loop(0, count)
    def _(t):
        cc, j, rel = offset(t)

        @pl.when(rel < own_rows + XM)
        def _():
            fetch(t, cc, j).wait()
            value = mm(jnp.concatenate([tv[t, 0], tv[t, 1]], axis=1), maps[cc])
            turn = lax.rem(rel, ALIGN)
            low = pl.multiple_of(rel - turn, ALIGN)
            acc[pl.ds(low, XM), :] += jnp.where(slot >= turn, value, 0.0)
            acc[pl.ds(pl.multiple_of(low + XM, ALIGN), ALIGN), :] += jnp.where(
                edge < turn, value[:ALIGN], 0.0
            )

    chunk = own_rows // OUT_CHUNKS
    copies = []
    for k in range(OUT_CHUNKS):
        rows = pl.ds(k * chunk, chunk)
        src = pl.ds(XM + k * chunk, chunk)
        stage[0, rows, :] = acc[src, :oc].astype(BF16)
        stage[1, rows, :] = acc[src, oc:].astype(BF16)
        copy = pltpu.make_async_copy(stage.at[:, rows, :], out.at[:, rows, :], osem.at[k])
        copy.start()
        copies.append(copy)
    for copy in copies:
        copy.wait()


def body(prepared, sub_off, fac_off, win_col, vis_weights):
    nf = fac_off.shape[0]
    ncol = lax.axis_size("col")
    facet_strip = prepared[0]
    facet_len, width = facet_strip.shape[1:]
    strip_blocks = facet_strip.reshape(2, facet_len // XM, XM, width)
    weights = vis_weights[0]
    xa = weights.shape[1]
    oc = width * ncol // 2
    own_rows = facet_len // ncol
    starts = sub_off[:, 0]
    lanes = -(-nf // 128) * 128

    forward, backward = window_tables(XM)
    q_table = stacked(*dft(xa, -1.0, 1.0 / math.sqrt(nf * XM)), 0)
    out_map = stacked(*dft(oc, 1.0, 1.0 / math.sqrt(2 * oc)), 1)

    smem = pl.BlockSpec(memory_space=pltpu.SMEM)
    vmem = pl.BlockSpec(memory_space=pltpu.VMEM)
    hbm = pl.BlockSpec(memory_space=pl.ANY)
    dma = pltpu.SemaphoreType.DMA
    halves = pltpu.VMEM((2, nf, XM, width), BF16)
    maps = (ncol, 2 * width, 2 * oc)
    terms, starts_all, maps_all = pl.pallas_call(
        functools.partial(exchange_kernel, nf, ncol),
        out_shape=(
            jax.ShapeDtypeStruct((ncol, nf, 2, XM, width), BF16),
            jax.ShapeDtypeStruct((ncol, 8, lanes), jnp.int32),
            jax.ShapeDtypeStruct(maps, BF16),
        ),
        in_specs=[smem, smem, hbm, hbm, vmem, vmem, vmem, hbm, hbm],
        out_specs=(hbm, hbm, hbm),
        scratch_shapes=[
            pltpu.VMEM(strip_blocks.shape, BF16),
            pltpu.VMEM(q_table.shape, BF16),
            pltpu.VMEM(weights.shape, BF16),
            halves,
            halves,
            pltpu.VMEM((xa, width), F32),
            pltpu.VMEM((xa, width), BF16),
            halves,
            pltpu.VMEM((nf, 2 * XM, xa), BF16),
            pltpu.VMEM(maps, BF16),
            pltpu.VMEM((8, lanes), jnp.int32),
            pltpu.VMEM(out_map.shape, BF16),
            pltpu.VMEM((2, 2, xa, width), F32),
            dma((CHUNKS + 7,)), dma((2, nf)), dma((2, nf)), dma((2, nf)),
            dma((ncol, nf, 2)), dma((ncol, nf, 2)), dma((ncol, nf, 2)), dma((ncol,)), dma((ncol,)),
        ],
        compiler_params=pltpu.CompilerParams(collective_id=0, has_side_effects=True),
        name="exchange",
    )(
        starts, fac_off, strip_blocks, weights, jnp.asarray(forward), jnp.asarray(backward),
        win_col, jnp.asarray(out_map), jnp.asarray(q_table),
    )
    out = pl.pallas_call(
        functools.partial(finish_kernel, nf, ncol),
        out_shape=jax.ShapeDtypeStruct((2, own_rows, oc), BF16),
        in_specs=[smem, hbm, hbm],
        out_specs=hbm,
        scratch_shapes=[
            pltpu.VMEM((ncol * nf, 2, XM, width), BF16),
            pltpu.VMEM((own_rows + 2 * XM + ALIGN, 2 * oc), F32),
            pltpu.VMEM(maps, BF16),
            pltpu.VMEM((2, own_rows, oc), BF16),
            dma((ncol * nf + 1,)),
            dma((OUT_CHUNKS,)),
        ],
        name="finish",
    )(starts_all, terms, maps_all)
    return out[None]


def solution(mesh):
    in_specs = (
        P("facet", None, None, "col"),
        P(None, "col"),
        P(),
        P(),
        P("facet", None, None, "col"),
    )
    out_specs = P("facet", None, "col", None)
    return jax.shard_map(body, mesh=mesh, in_specs=in_specs, out_specs=out_specs, check_vma=False)
```

time: 53.9 us -> 52.6 us (0.976)
  the two profiles are of different devices: /device:TPU:1 before, /device:TPU:0 now
where the time goes in v2:
time: 52.6 us; the launch traced here: 52.3 us
  Pallas kernels  52.2 us (99%)
    pallas_call x1, Pallas kernels, body(): pl.pallas_call(functools.partial(exchange_kernel, nf, ncol), out_shape=(j...  46.1 us
    pallas_call x1, Pallas kernels, body(): pl.pallas_call(functools.partial(finish_kernel, nf, ncol), out_shape=jax....  6.13 us

profile of v2, /device:TPU:0, one launch (start us, length us, event | category | flops | bytes accessed | tf_op | source)
XLA Modules:
  0.0 52.3 jit_solution(12581024301148772196)
XLA Ops:
  0.0 46.1 %exchange.1 = (bf16[4,8,2,128,128]{4,3,2,1,0:T(8,128)(2,1)}, s32[4,8,128]{2,1,0:T(8,128)}, bf16[4,256,512]{2,1,0:T(8,128)(2,1)}) custom-call(s32[8]{0:T(128)} %bitcast.6, s32[8]{0:T(128)} %fac.1, bf16[2,64,128,128]{3,2,1,0:T(8,128)(2,1)} %bitcast.4, bf16[2,512,128]{2,1,0:T(8,128)(2,1)} %bitcast.5, bf16[256,128]{1,0:T(8,128)(2,1)} %constant.8.clone.fwd, ...), custom_call_target="tpu_custom_call" | custom-call | tf_op jit(solution)/shard_map/exchange/pallas_call | solution.py:423
  46.1 6.1 %finish.1 = bf16[2,2048,256]{2,1,0:T(8,128)(2,1)} custom-call(s32[4,8,128]{2,1,0:T(8,128)} %get-tuple-element.8.starts_all, bf16[4,8,2,128,128]{4,3,2,1,0:T(8,128)(2,1)} %get-tuple-element.9.terms, bf16[4,256,512]{2,1,0:T(8,128)(2,1)} %get-tuple-element.10.maps_in), custom_call_target="tpu_custom_call" | custom-call | tf_op jit(solution)/shard_map/finish/pallas_call | solution.py:455
